TPU v7x, 32 devices: a whole 2x2x4 slice. The times are simulated.
32 devices in a mesh: freq: 4 (over x, core), rows: 8 (over z, y).
Axes of the slice: x: 2, y: 2, z: 4, core: 2. Of those that a mesh axis runs over, the one named last changes fastest.
Arguments:
- time_loads: float32 [256, 192, 2048], P('freq', None, 'rows'), may hold values from -6 to 6
- factor: float32 [16, 2, 2048, 2048], P('freq', None, 'rows'), may hold values from -0.09375 to 0.09375
- diag_inverse: float32 [16, 2, 2048, 256], P('freq', None, 'rows'), may hold values from -0.25 to 0.25
- pivot_order: int32 [8], replicated, may hold values from 0 to 7, each once
Outputs:
- solution: float32 [16, 2, 192, 2048], P('freq', None, None, 'rows')
Inputs may be any that keep to these rules, and one draw needn't show every extreme that they name: `pivot_order`: a permutation of the 8 row blocks.
All inputs are finite; a program needn't handle non-finite values.
Results may differ from a plain program's by a relative error of at most 0.0001.
Values sent between devices are 32-bit elements; how exact they have to be, the bound alone decides.
A program may use at most 128 MiB of HBM per device.

v0:
```python
import jax
import jax.numpy as jnp
from jax import lax
from jax.sharding import PartitionSpec as P

FREQS = 16
STEPS = 256


def broadcast(value, axis, source):
    kept = jnp.where(lax.axis_index(axis) == source, value, 0).astype(value.dtype)
    return lax.psum(kept, axis)


def tables(count, length):
    freq_range = jnp.arange(count, dtype=jnp.float32)
    step_range = jnp.arange(length, dtype=jnp.float32)
    angles = 2.0 * jnp.pi * (freq_range[:, None] * step_range[None, :] % length) / length
    damping = jnp.exp(step_range * (jnp.log(0.1) / length))
    return (jnp.cos(angles) * damping[None, :], -jnp.sin(angles) * damping[None, :])


def product(matrix, vector):
    return jnp.einsum("fab,fcb->fca", matrix, vector, precision=lax.Precision.HIGHEST)


def complex_apply(matrix, vector):
    matrix_real, matrix_imag = (matrix[:, 0], matrix[:, 1])
    vector_real, vector_imag = (vector[:, 0], vector[:, 1])
    real_part = product(matrix_real, vector_real) - product(matrix_imag, vector_imag)
    imag_part = product(matrix_real, vector_imag) + product(matrix_imag, vector_real)
    return jnp.stack([real_part, imag_part], axis=1)


def body(time_loads, factor, diag_inverse, pivot_order):
    cosine_table, sine_table = tables(FREQS, STEPS)
    local_freqs = factor.shape[0]
    local_steps = time_loads.shape[0]
    offset = lax.axis_index("freq") * local_steps
    cosine_part = lax.dynamic_slice(
        cosine_table, (0, offset), (local_freqs * lax.axis_size("freq"), local_steps)
    )
    sine_part = lax.dynamic_slice(
        sine_table, (0, offset), (local_freqs * lax.axis_size("freq"), local_steps)
    )
    spectra = lax.psum_scatter(
        jnp.stack(
            [
                jnp.einsum("fn,ncr->fcr", cosine_part, time_loads, precision=lax.Precision.HIGHEST),
                jnp.einsum("fn,ncr->fcr", sine_part, time_loads, precision=lax.Precision.HIGHEST),
            ],
            axis=1,
        ),
        "freq",
        scatter_dimension=0,
        tiled=True,
    )
    my_block = lax.axis_index("rows")
    blocks = lax.axis_size("rows")
    block_rows = diag_inverse.shape[3]

    def advance(turn, state_pair):
        residual, solution = state_pair
        pivot_index = pivot_order[turn]
        is_owner = pivot_index == my_block
        solved = lax.cond(
            is_owner,
            lambda current: complex_apply(diag_inverse, current),
            lambda current: jnp.zeros_like(current),
            residual,
        )
        pivot = broadcast(solved, "rows", pivot_index)
        solution = jnp.where(is_owner, pivot, solution)
        column = lax.dynamic_slice_in_dim(factor, pivot_index * block_rows, block_rows, 3)
        residual = residual - complex_apply(column, pivot)
        return (residual, solution)

    residual, solution = lax.fori_loop(0, blocks, advance, (spectra, jnp.zeros_like(spectra)))
    return solution


def solution(mesh):
    placed = (
        P("freq", None, "rows"),
        P("freq", None, "rows", None),
        P("freq", None, "rows", None),
        P(),
    )
    return jax.shard_map(
        body, mesh=mesh, in_specs=placed, out_specs=P("freq", None, None, "rows"), check_vma=False
    )
```

profile of v0, /device:TPU:0, one launch (start us, length us, event | category | flops | bytes accessed | tf_op | source)
XLA Modules:
  0.0 998.1 jit_solution(14267200974558507674)
XLA Ops:
  6.7 18.0 %fusion.32 = f32[16,1,192,256]{3,0,2,1:T(8,128)S(1)} fusion(f32[64,192,256]{2,1,0:T(8,128)} %param.8, f32[16,256]{1,0:T(8,128)S(1)} %fusion.38, s32[]{:T(128)S(6)} %select_n.73, f32[64]{0:T(128)S(1)} %dynamic-slice.2), kind=kOutput, calls=%fused_computation.45 | convolution fusion | flops 603980800 | bytes 15737348 | tf_op jit(solution)/shard_map/fn,ncr->fcr/dot_general | solution.py:49
  24.6 13.5 %fusion.35 = f32[16,1,192,256]{3,0,2,1:T(8,128)S(1)} fusion(f32[64,192,256]{2,1,0:T(8,128)S(1)} %copy-done.4, f32[16,256]{1,0:T(8,128)S(1)} %fusion.38, s32[]{:T(128)S(6)} %select_n.73, f32[64]{0:T(128)S(1)} %dynamic-slice.2), kind=kOutput, calls=%fused_computation.46 | convolution fusion | flops 603981824 | bytes 15737348 | tf_op jit(solution)/shard_map/fn,ncr->fcr/dot_general | solution.py:50
  38.9 6.3 copy.13
  48.3 58.6 %reduce-scatter.2.cloned.1.call-done = f32[4,2,192,256]{3,2,1,0:T(8,128)} async-done(((f32[16,2,192,256]{3,2,1,0:T(8,128)}), f32[4,2,192,256]{3,2,1,0:T(8,128)}) %reduce-scatter.2.cloned.1.call-update) | async-done | bytes 1572880 | tf_op jit(solution)/shard_map/reduce_scatter | solution.py:46
  108.5 880.4 %while.18 = (s32[]{:T(128)}, f32[4,2,192,256]{3,2,0,1:T(8,128)S(1)}, f32[4,2,192,256]{3,2,0,1:T(8,128)}, s32[8]{0:T(128)S(1)}, s32[]{:T(128)}, /*index=5*/f32[4,...) while((s32[]{:T(128)}, ...), condition=%wide.region_5.6_spmd.clone, body=%wide.region_1.5_spmd.clone.sunk | while | flops 4835377152 | bytes 76546488 | solution.py:78
  112.5 93.3 %all-reduce.2.cloned.1.call-done = f32[4,2,192,256]{3,2,0,1:T(8,128)} async-done(((f32[4,2,192,256]{3,2,0,1:T(8,128)}), f32[4,2,192,256]{3,2,0,1:T(8,128)}) %all-reduce.2.cloned.1.call-update) | async-done | bytes 1572880 | tf_op jit(solution)/shard_map/while/body/eval_jaxpr/psum | solution.py:12
  205.8 2.8 fusion.61
  208.6 2.5 fusion.59
  211.1 2.5 fusion.62
  213.6 2.6 fusion.60
  222.4 93.2 %all-reduce.2.cloned.1.call-done = f32[4,2,192,256]{3,2,0,1:T(8,128)} async-done(((f32[4,2,192,256]{3,2,0,1:T(8,128)}), f32[4,2,192,256]{3,2,0,1:T(8,128)}) %all-reduce.2.cloned.1.call-update) | async-done | bytes 1572880 | tf_op jit(solution)/shard_map/while/body/eval_jaxpr/psum | solution.py:12
  315.6 2.8 fusion.61
  318.4 2.5 fusion.59
  320.9 2.5 fusion.62
  323.4 2.6 fusion.60
  330.1 6.5 conditional.3
  330.1 2.6 fusion.6
  338.5 86.0 %all-reduce.2.cloned.1.call-done = f32[4,2,192,256]{3,2,0,1:T(8,128)} async-done(((f32[4,2,192,256]{3,2,0,1:T(8,128)}), f32[4,2,192,256]{3,2,0,1:T(8,128)}) %all-reduce.2.cloned.1.call-update) | async-done | bytes 1572880 | tf_op jit(solution)/shard_map/while/body/eval_jaxpr/psum | solution.py:12
  424.5 2.8 fusion.61
  427.4 2.5 fusion.59
  429.9 2.5 fusion.62
  432.4 2.6 fusion.60
  441.1 94.4 %all-reduce.2.cloned.1.call-done = f32[4,2,192,256]{3,2,0,1:T(8,128)} async-done(((f32[4,2,192,256]{3,2,0,1:T(8,128)}), f32[4,2,192,256]{3,2,0,1:T(8,128)}) %all-reduce.2.cloned.1.call-update) | async-done | bytes 1572880 | tf_op jit(solution)/shard_map/while/body/eval_jaxpr/psum | solution.py:12
  535.5 2.8 fusion.61
  538.3 2.5 fusion.59
  540.8 2.5 fusion.62
  543.3 2.6 fusion.60
  552.1 93.5 %all-reduce.2.cloned.1.call-done = f32[4,2,192,256]{3,2,0,1:T(8,128)} async-done(((f32[4,2,192,256]{3,2,0,1:T(8,128)}), f32[4,2,192,256]{3,2,0,1:T(8,128)}) %all-reduce.2.cloned.1.call-update) | async-done | bytes 1572880 | tf_op jit(solution)/shard_map/while/body/eval_jaxpr/psum | solution.py:12
  645.5 2.8 fusion.61
  648.4 2.5 fusion.59
  650.9 2.5 fusion.62
  653.4 2.6 fusion.60
  662.1 93.1 %all-reduce.2.cloned.1.call-done = f32[4,2,192,256]{3,2,0,1:T(8,128)} async-done(((f32[4,2,192,256]{3,2,0,1:T(8,128)}), f32[4,2,192,256]{3,2,0,1:T(8,128)}) %all-reduce.2.cloned.1.call-update) | async-done | bytes 1572880 | tf_op jit(solution)/shard_map/while/body/eval_jaxpr/psum | solution.py:12
  755.2 2.8 fusion.61
  758.1 2.5 fusion.59
  760.6 2.5 fusion.62
  763.1 2.6 fusion.60
  771.8 93.5 %all-reduce.2.cloned.1.call-done = f32[4,2,192,256]{3,2,0,1:T(8,128)} async-done(((f32[4,2,192,256]{3,2,0,1:T(8,128)}), f32[4,2,192,256]{3,2,0,1:T(8,128)}) %all-reduce.2.cloned.1.call-update) | async-done | bytes 1572880 | tf_op jit(solution)/shard_map/while/body/eval_jaxpr/psum | solution.py:12
  865.3 2.8 fusion.61
  868.1 2.5 fusion.59
  870.6 2.5 fusion.62
  873.1 2.6 fusion.60
  881.9 94.4 %all-reduce.2.cloned.1.call-done = f32[4,2,192,256]{3,2,0,1:T(8,128)} async-done(((f32[4,2,192,256]{3,2,0,1:T(8,128)}), f32[4,2,192,256]{3,2,0,1:T(8,128)}) %all-reduce.2.cloned.1.call-update) | async-done | bytes 1572880 | tf_op jit(solution)/shard_map/while/body/eval_jaxpr/psum | solution.py:12
  976.2 2.8 fusion.61
  979.1 2.5 fusion.59
  981.6 2.5 fusion.62
  984.1 2.6 fusion.60
  988.9 2.7 copy.17
  (123 shorter events, 44.2 us)
Async XLA Ops:
  6.5 100.4 %reduce-scatter.2.cloned.1.call-start = ((), (), s32[]{:S(2)}) async-start(), calls=%async_computation.1 | async-start | bytes 7864320 | tf_op jit(solution)/shard_map/reduce_scatter | solution.py:46
  6.7 18.0 %copy-start.4 = (f32[64,192,256]{2,1,0:T(8,128)S(1)}, f32[64,192,256]{2,1,0:T(8,128)}, u32[]{:S(2)}) copy-start(f32[64,192,256]{2,1,0:T(8,128)} %param.8) | copy-start | bytes 37748740
  45.1 1.6 copy-start.5
  48.3 60.2 %copy-start.6 = (s32[8]{0:T(128)S(1)}, s32[8]{0:T(128)}, u32[]{:S(2)}) copy-start(s32[8]{0:T(128)} %param.11) | copy-start | bytes 100
  108.5 97.3 %all-reduce.2.cloned.1.call-start = ((), (), s32[]{:S(2)}) async-start(), calls=%async_computation.2 | async-start | bytes 3145728 | tf_op jit(solution)/shard_map/while/body/eval_jaxpr/psum | solution.py:12
  205.8 2.8 copy-start
  213.6 2.6 copy-start.2
  217.2 1.2 copy-start.3
  218.4 97.2 %all-reduce.2.cloned.1.call-start = ((), (), s32[]{:S(2)}) async-start(), calls=%async_computation.2 | async-start | bytes 3145728 | tf_op jit(solution)/shard_map/while/body/eval_jaxpr/psum | solution.py:12
  315.6 2.8 copy-start
  323.4 2.6 copy-start.2
  327.0 1.2 copy-start.3
  328.2 96.3 %all-reduce.2.cloned.1.call-start = ((), (), s32[]{:S(2)}) async-start(), calls=%async_computation.2 | async-start | bytes 3145728 | tf_op jit(solution)/shard_map/while/body/eval_jaxpr/psum | solution.py:12
  330.1 2.6 copy-start.1
  424.5 2.8 copy-start
  432.4 2.6 copy-start.2
  436.0 1.2 copy-start.3
  437.2 98.3 %all-reduce.2.cloned.1.call-start = ((), (), s32[]{:S(2)}) async-start(), calls=%async_computation.2 | async-start | bytes 3145728 | tf_op jit(solution)/shard_map/while/body/eval_jaxpr/psum | solution.py:12
  535.5 2.8 copy-start
  543.3 2.6 copy-start.2
  546.9 1.2 copy-start.3
  548.1 97.4 %all-reduce.2.cloned.1.call-start = ((), (), s32[]{:S(2)}) async-start(), calls=%async_computation.2 | async-start | bytes 3145728 | tf_op jit(solution)/shard_map/while/body/eval_jaxpr/psum | solution.py:12
  645.5 2.8 copy-start
  653.4 2.6 copy-start.2
  657.0 1.2 copy-start.3
  658.2 97.0 %all-reduce.2.cloned.1.call-start = ((), (), s32[]{:S(2)}) async-start(), calls=%async_computation.2 | async-start | bytes 3145728 | tf_op jit(solution)/shard_map/while/body/eval_jaxpr/psum | solution.py:12
  755.2 2.8 copy-start
  763.1 2.6 copy-start.2
  766.7 1.2 copy-start.3
  767.9 97.4 %all-reduce.2.cloned.1.call-start = ((), (), s32[]{:S(2)}) async-start(), calls=%async_computation.2 | async-start | bytes 3145728 | tf_op jit(solution)/shard_map/while/body/eval_jaxpr/psum | solution.py:12
  865.3 2.8 copy-start
  873.1 2.6 copy-start.2
  876.7 1.2 copy-start.3
  877.9 98.3 %all-reduce.2.cloned.1.call-start = ((), (), s32[]{:S(2)}) async-start(), calls=%async_computation.2 | async-start | bytes 3145728 | tf_op jit(solution)/shard_map/while/body/eval_jaxpr/psum | solution.py:12
  976.2 2.8 copy-start
  984.1 2.6 copy-start.2
  987.7 1.2 copy-start.3
Sparse Core Ops, SparseCore 0:
  45.3 61.5 reduce-scatter.1
  112.8 92.8 all-reduce.1
  222.7 92.8 all-reduce.1
  338.0 86.4 all-reduce.1
  441.2 94.2 all-reduce.1
  552.1 93.3 all-reduce.1
  662.5 92.6 all-reduce.1
  772.2 93.0 all-reduce.1
  882.2 93.9 all-reduce.1
where the time goes:
time: 999 us; the launch traced here: 998 us
  waiting for transfers between devices  800 us (80%)
  matrix products  121 us (12%)
  local copies, waits for them, and re-layouts  29.1 us (3%)
  other arithmetic  19.2 us (2%)
  loops' own time  15.6 us (2%)
  between operations  13.1 us (1%)
    psum x8, waiting for transfers between devices, broadcast(): return lax.psum(kept, axis)  741 us
    dot_general x36, matrix products, product(): jnp.einsum('fab,fcb->fca', matrix, vector, precision=lax.Precision.HIGHEST)  89.5 us
    reduce_scatter x1, waiting for transfers between devices, body(): lax.psum_scatter(jnp.stack([jnp.einsum('fn,ncr->fcr', cosine_part, time_l...  58.6 us
  transfers between devices with their start and end apart: 9, of which 9 were waited for; matrix products, arithmetic and copies ran while one was open for 0% of the time, Pallas kernels for 0%

commit v1 on v0

--- a/solution.py
+++ b/solution.py
@@ -8,8 +8,13 @@
 
 
 def broadcast(value, axis, source):
+
+    def make_entries(my_data, lane_axis):
+        e_now = jax.lax.all_gather(my_data, axis_name=lane_axis)
+        return jnp.sum(e_now, 0)
+
     kept = jnp.where(lax.axis_index(axis) == source, value, 0).astype(value.dtype)
-    return lax.psum(kept, axis)
+    return make_entries(kept, lane_axis=axis)
 
 
 def tables(count, length):

time: 999 us -> 1730 us (1.73)
  waiting for transfers between devices: 800 us -> 1490 us
  other arithmetic: 19.2 us -> 64 us
    all_gather x0 -> x8, waiting for transfers between devices: none -> 1430 us  [make_entries(): e_now = jax.lax.all_gather(my_data, axis_name=lane_axis)]
    psum x8 -> x0, waiting for transfers between devices: 741 us -> none  [broadcast(): return lax.psum(kept, axis)]
    reduce_sum x0 -> x8, other arithmetic: none -> 44.9 us  [make_entries(): return jnp.sum(e_now, 0)]
where the time goes in v1:
time: 1730 us
  waiting for transfers between devices  1490 us (86%)
  matrix products  118 us (7%)
  other arithmetic  64 us (4%)
  local copies, waits for them, and re-layouts  28.3 us (2%)
    all_gather x8, waiting for transfers between devices, make_entries(): e_now = jax.lax.all_gather(my_data, axis_name=lane_axis)  1430 us
    dot_general x36, matrix products, product(): jnp.einsum('fab,fcb->fca', matrix, vector, precision=lax.Precision.HIGHEST)  86.7 us
    reduce_scatter x1, waiting for transfers between devices, body(): lax.psum_scatter(jnp.stack([jnp.einsum('fn,ncr->fcr', cosine_part, time_l...  58.6 us
    reduce_sum x8, other arithmetic, make_entries(): return jnp.sum(e_now, 0)  44.9 us
  transfers between devices with their start and end apart: 9, of which 9 were waited for; matrix products, arithmetic and copies ran while one was open for 0% of the time, Pallas kernels for 0%

profile of v1, /device:TPU:0, one launch (start us, length us, event | category | flops | bytes accessed | tf_op | source)
XLA Modules:
  0.0 1727.7 jit_solution(16391901214046768033)
XLA Ops:
  6.7 18.0 %fusion.32 = f32[16,1,192,256]{3,0,2,1:T(8,128)S(1)} fusion(f32[64,192,256]{2,1,0:T(8,128)} %param.8, f32[16,256]{1,0:T(8,128)S(1)} %fusion.38, s32[]{:T(128)S(6)} %select_n.73, f32[64]{0:T(128)S(1)} %dynamic-slice.2), kind=kOutput, calls=%fused_computation.45 | convolution fusion | flops 603980800 | bytes 15737348 | tf_op jit(solution)/shard_map/fn,ncr->fcr/dot_general | solution.py:54
  24.6 13.5 fusion.35
  38.9 6.3 copy.13
  48.3 58.6 %reduce-scatter.2.cloned.1.call-done = f32[4,2,192,256]{3,2,1,0:T(8,128)} async-done(((f32[16,2,192,256]{3,2,1,0:T(8,128)}), f32[4,2,192,256]{3,2,1,0:T(8,128)}) %reduce-scatter.2.cloned.1.call-update) | async-done | bytes 1572880 | tf_op jit(solution)/shard_map/reduce_scatter | solution.py:51
  108.5 1610.0 %while.18 = (s32[]{:T(128)}, f32[4,2,192,256]{3,2,0,1:T(8,128)S(1)}, f32[4,2,192,256]{3,2,0,1:T(8,128)}, s32[8]{0:T(128)S(1)}, s32[]{:T(128)}, /*index=5*/f32[4,...) while((s32[]{:T(128)}, ...), condition=%wide.region_5.6_spmd.clone, body=%wide.region_1.5_spmd.clone.sunk | while | flops 4837736448 | bytes 117440944 | solution.py:83
  112.3 180.2 %all-gather.6.cloned.1.call-done = f32[32,2,192,256]{3,2,0,1:T(8,128)} async-done(((f32[4,2,192,256]{3,2,0,1:T(8,128)}), f32[32,2,192,256]{3,2,0,1:T(8,128)}) %all-gather.6.cloned.1.call-update) | async-done | bytes 12582928 | tf_op jit(solution)/shard_map/while/body/eval_jaxpr/all_gather | solution.py:13
  292.4 5.6 reduce_sum.18
  298.1 2.5 fusion.61
  303.0 2.5 fusion.62
  305.5 2.6 fusion.60
  314.0 179.2 %all-gather.6.cloned.1.call-done = f32[32,2,192,256]{3,2,0,1:T(8,128)} async-done(((f32[4,2,192,256]{3,2,0,1:T(8,128)}), f32[32,2,192,256]{3,2,0,1:T(8,128)}) %all-gather.6.cloned.1.call-update) | async-done | bytes 12582928 | tf_op jit(solution)/shard_map/while/body/eval_jaxpr/all_gather | solution.py:13
  493.2 5.6 reduce_sum.18
  501.3 2.5 fusion.59
  503.8 2.5 fusion.62
  506.3 2.6 fusion.60
  512.8 6.5 conditional.3
  512.8 2.6 fusion.6
  521.1 172.9 %all-gather.6.cloned.1.call-done = f32[32,2,192,256]{3,2,0,1:T(8,128)} async-done(((f32[4,2,192,256]{3,2,0,1:T(8,128)}), f32[32,2,192,256]{3,2,0,1:T(8,128)}) %all-gather.6.cloned.1.call-update) | async-done | bytes 12582928 | tf_op jit(solution)/shard_map/while/body/eval_jaxpr/all_gather | solution.py:13
  694.0 5.6 reduce_sum.18
  699.6 2.5 fusion.61
  702.1 2.5 fusion.59
  704.6 2.5 fusion.62
  707.1 2.6 fusion.60
  715.6 180.1 %all-gather.6.cloned.1.call-done = f32[32,2,192,256]{3,2,0,1:T(8,128)} async-done(((f32[4,2,192,256]{3,2,0,1:T(8,128)}), f32[32,2,192,256]{3,2,0,1:T(8,128)}) %all-gather.6.cloned.1.call-update) | async-done | bytes 12582928 | tf_op jit(solution)/shard_map/while/body/eval_jaxpr/all_gather | solution.py:13
  895.7 5.6 reduce_sum.18
  903.8 2.5 fusion.59
  906.2 2.5 fusion.62
  908.7 2.6 fusion.60
  917.2 180.2 %all-gather.6.cloned.1.call-done = f32[32,2,192,256]{3,2,0,1:T(8,128)} async-done(((f32[4,2,192,256]{3,2,0,1:T(8,128)}), f32[32,2,192,256]{3,2,0,1:T(8,128)}) %all-gather.6.cloned.1.call-update) | async-done | bytes 12582928 | tf_op jit(solution)/shard_map/while/body/eval_jaxpr/all_gather | solution.py:13
  1097.4 5.6 reduce_sum.18
  1103.0 2.5 fusion.61
  1108.0 2.5 fusion.62
  1110.5 2.6 fusion.60
  1119.0 178.3 %all-gather.6.cloned.1.call-done = f32[32,2,192,256]{3,2,0,1:T(8,128)} async-done(((f32[4,2,192,256]{3,2,0,1:T(8,128)}), f32[32,2,192,256]{3,2,0,1:T(8,128)}) %all-gather.6.cloned.1.call-update) | async-done | bytes 12582928 | tf_op jit(solution)/shard_map/while/body/eval_jaxpr/all_gather | solution.py:13
  1297.3 5.6 reduce_sum.18
  1307.9 2.5 fusion.62
  1310.4 2.6 fusion.60
  1318.8 180.1 %all-gather.6.cloned.1.call-done = f32[32,2,192,256]{3,2,0,1:T(8,128)} async-done(((f32[4,2,192,256]{3,2,0,1:T(8,128)}), f32[32,2,192,256]{3,2,0,1:T(8,128)}) %all-gather.6.cloned.1.call-update) | async-done | bytes 12582928 | tf_op jit(solution)/shard_map/while/body/eval_jaxpr/all_gather | solution.py:13
  1498.9 5.6 reduce_sum.18
  1507.0 2.5 fusion.59
  1509.5 2.5 fusion.62
  1512.0 2.6 fusion.60
  1520.5 180.2 %all-gather.6.cloned.1.call-done = f32[32,2,192,256]{3,2,0,1:T(8,128)} async-done(((f32[4,2,192,256]{3,2,0,1:T(8,128)}), f32[32,2,192,256]{3,2,0,1:T(8,128)}) %all-gather.6.cloned.1.call-update) | async-done | bytes 12582928 | tf_op jit(solution)/shard_map/while/body/eval_jaxpr/all_gather | solution.py:13
  1700.7 5.6 reduce_sum.18
  1708.8 2.5 fusion.59
  1711.2 2.5 fusion.62
  1713.7 2.6 fusion.60
  1718.5 2.7 copy.17
  (115 shorter events, 63.3 us)
Async XLA Ops:
  6.5 100.4 %reduce-scatter.2.cloned.1.call-start = ((), (), s32[]{:S(2)}) async-start(), calls=%async_computation.1 | async-start | bytes 7864320 | tf_op jit(solution)/shard_map/reduce_scatter | solution.py:51
  6.7 18.0 %copy-start.3 = (f32[64,192,256]{2,1,0:T(8,128)S(1)}, f32[64,192,256]{2,1,0:T(8,128)}, u32[]{:S(2)}) copy-start(f32[64,192,256]{2,1,0:T(8,128)} %param.8) | copy-start | bytes 37748740
  45.2 1.6 copy-start.4
  48.3 60.2 %copy-start.5 = (s32[8]{0:T(128)S(1)}, s32[8]{0:T(128)}, u32[]{:S(2)}) copy-start(s32[8]{0:T(128)} %param.11) | copy-start | bytes 100
  108.5 183.9 %all-gather.6.cloned.1.call-start = ((), (), s32[]{:S(2)}) async-start(), calls=%async_computation.2 | async-start | bytes 14155776 | tf_op jit(solution)/shard_map/while/body/eval_jaxpr/all_gather | solution.py:13
  305.5 2.6 copy-start.1
  309.1 1.2 copy-start.2
  310.3 182.9 %all-gather.6.cloned.1.call-start = ((), (), s32[]{:S(2)}) async-start(), calls=%async_computation.2 | async-start | bytes 14155776 | tf_op jit(solution)/shard_map/while/body/eval_jaxpr/all_gather | solution.py:13
  506.3 2.6 copy-start.1
  509.9 1.2 copy-start.2
  511.1 182.9 %all-gather.6.cloned.1.call-start = ((), (), s32[]{:S(2)}) async-start(), calls=%async_computation.2 | async-start | bytes 14155776 | tf_op jit(solution)/shard_map/while/body/eval_jaxpr/all_gather | solution.py:13
  512.8 2.6 copy-start
  707.1 2.6 copy-start.1
  710.7 1.2 copy-start.2
  711.9 183.8 %all-gather.6.cloned.1.call-start = ((), (), s32[]{:S(2)}) async-start(), calls=%async_computation.2 | async-start | bytes 14155776 | tf_op jit(solution)/shard_map/while/body/eval_jaxpr/all_gather | solution.py:13
  908.7 2.6 copy-start.1
  912.4 1.2 copy-start.2
  913.5 183.9 %all-gather.6.cloned.1.call-start = ((), (), s32[]{:S(2)}) async-start(), calls=%async_computation.2 | async-start | bytes 14155776 | tf_op jit(solution)/shard_map/while/body/eval_jaxpr/all_gather | solution.py:13
  1110.5 2.6 copy-start.1
  1114.1 1.2 copy-start.2
  1115.3 182.0 %all-gather.6.cloned.1.call-start = ((), (), s32[]{:S(2)}) async-start(), calls=%async_computation.2 | async-start | bytes 14155776 | tf_op jit(solution)/shard_map/while/body/eval_jaxpr/all_gather | solution.py:13
  1310.4 2.6 copy-start.1
  1314.0 1.2 copy-start.2
  1315.1 183.8 %all-gather.6.cloned.1.call-start = ((), (), s32[]{:S(2)}) async-start(), calls=%async_computation.2 | async-start | bytes 14155776 | tf_op jit(solution)/shard_map/while/body/eval_jaxpr/all_gather | solution.py:13
  1512.0 2.6 copy-start.1
  1515.6 1.2 copy-start.2
  1516.8 183.9 %all-gather.6.cloned.1.call-start = ((), (), s32[]{:S(2)}) async-start(), calls=%async_computation.2 | async-start | bytes 14155776 | tf_op jit(solution)/shard_map/while/body/eval_jaxpr/all_gather | solution.py:13
  1713.7 2.6 copy-start.1
  1717.4 1.2 copy-start.2
Sparse Core Ops, SparseCore 0:
  45.3 61.5 reduce-scatter.1
  111.8 180.5 all-gather.5
  313.6 179.6 all-gather.5
  520.7 173.3 all-gather.5
  715.2 180.4 all-gather.5
  916.8 180.5 all-gather.5
  1118.5 178.7 all-gather.5
  1318.4 180.4 all-gather.5
  1520.0 180.5 all-gather.5
